TPU v7x, 256 devices: a whole 4x4x8 slice. The times are simulated.
256 devices in a mesh: section: 16 (over z_lo, y), dp: 16 (over x, z_hi, core).
Axes of the slice: x: 4, y: 4, z: 8 (z_hi: 2, z_lo: 4; z = z_hi * 4 + z_lo), core: 2. Of those that a mesh axis runs over, the one named last changes fastest.
Arguments:
- enc_state: bfloat16 [16, 512, 4096], P('section', 'dp'), may hold values from -1000 to 1000
- final_gain: float32 [4096], replicated, may hold values from 0.5 to 1.5
- queries: bfloat16 [16, 2048, 4096], P('section', 'dp'), may hold values from -60 to 60
- w_key: bfloat16 [16, 4096, 4096], P('section', None, 'dp'), may hold values from -0.09375 to 0.09375
- w_value: bfloat16 [16, 4096, 4096], P('section', None, 'dp'), may hold values from -0.09375 to 0.09375
- ctx_grad: bfloat16 [16, 2048, 4096], P('section', 'dp'), may hold values from -6 to 6
- mem_len: int32 [16], P('dp'), may hold values from 8 to 32, as said below
Outputs:
- query_grad: bfloat16 [16, 2048, 4096], P('section', 'dp')
- key_weight_grad: bfloat16 [16, 4096, 4096], P('section', None, 'dp')
- value_weight_grad: bfloat16 [16, 4096, 4096], P('section', None, 'dp')
- state_grad: bfloat16 [16, 512, 4096], P('section', 'dp')
- gain_grad: float32 [4096], replicated
Inputs may be any that keep to these rules, and one draw needn't show every extreme that they name: Sequence b's memory holds mem_len[b] valid tokens from position 0; in every draw some sequence has all 32.
All inputs are finite; a program needn't handle non-finite values.
Results may differ from a plain program's by a relative error of at most 0.028.
The roundings to bfloat16 on the way count: a program that leaves them out, or rounds other values in their place, can miss the bound.
Values may be sent and summed in bfloat16 or wider, within the bound.
A program may use at most 64 MiB of HBM per device.

v0:
```python
import jax
import jax.numpy as jnp
from jax import lax
from jax.sharding import PartitionSpec as P

HEAD_DIM = 256
epsilon = 1e-06


def broadcast(block, axis, holder):
    block = jnp.where(lax.axis_index(axis) == holder, block, jnp.zeros_like(block))
    return lax.psum(block, axis)


def on_device(enc_state, final_gain, queries, w_key, w_value, ctx_grad, mem_len):
    sections = lax.axis_size("section")
    replicas = lax.axis_size("dp")
    section_index = lax.axis_index("section")
    last_encoder = sections // 2 - 1
    is_decoder = (section_index > last_encoder).astype(jnp.float32)
    is_last = (section_index == last_encoder).astype(jnp.float32)
    src_len = enc_state.shape[1]
    tgt_len = queries.shape[1]
    local_width = w_key.shape[2]
    heads_here = local_width // HEAD_DIM
    score_scale = HEAD_DIM ** (-0.5)
    enc_rows = enc_state[0].astype(jnp.float32)
    inverse = lax.rsqrt(jnp.mean(enc_rows * enc_rows, axis=1, keepdims=True) + epsilon)
    normed = enc_rows * inverse
    memory = (normed * final_gain).astype(jnp.bfloat16)
    sent = broadcast(memory, "section", last_encoder)
    all_memory, all_len = (
        lax.all_gather(sent, "dp", axis=0, tiled=True),
        lax.all_gather(mem_len, "dp", axis=0, tiled=True),
    )
    w_both = jnp.concatenate([w_key[0], w_value[0]], axis=1)
    projected = jnp.dot(all_memory, w_both, preferred_element_type=jnp.float32).astype(jnp.bfloat16)
    key_rows = projected[:, :local_width].reshape(replicas, src_len, heads_here, HEAD_DIM)
    value_rows = projected[:, local_width:].reshape(replicas, src_len, heads_here, HEAD_DIM)
    query_heads, grad_heads = (
        lax.all_to_all(queries[0], "dp", split_axis=1, concat_axis=0, tiled=True),
        lax.all_to_all(ctx_grad[0], "dp", split_axis=1, concat_axis=0, tiled=True),
    )
    query_rows = query_heads.reshape(replicas, tgt_len, heads_here, HEAD_DIM)
    grad_rows = grad_heads.reshape(replicas, tgt_len, heads_here, HEAD_DIM)
    key_valid = jnp.arange(src_len, dtype=jnp.int32)[None, :] < all_len[:, None]
    scores = (
        jnp.einsum("btha,buha->bhut", query_rows, key_rows, preferred_element_type=jnp.float32)
        * score_scale
    )
    scores = jnp.where(key_valid[:, None, :, None], scores, -1e30)
    row_max = jnp.max(scores, axis=2, keepdims=True)
    exponent = jnp.exp(scores - row_max)
    probs = exponent / jnp.sum(exponent, axis=2, keepdims=True)
    probs_low = probs.astype(jnp.bfloat16)
    grad_probs = jnp.einsum(
        "btha,buha->bhut", grad_rows, value_rows, preferred_element_type=jnp.float32
    )
    row_delta = jnp.sum(probs * grad_probs, axis=2, keepdims=True)
    grad_scores = (probs * (grad_probs - row_delta) * score_scale).astype(jnp.bfloat16)
    query_grad_heads = (
        jnp.einsum("bhut,buha->btha", grad_scores, key_rows, preferred_element_type=jnp.float32)
        .astype(jnp.bfloat16)
        .reshape(replicas * tgt_len, local_width)
    )
    key_grad = (
        jnp.einsum("bhut,btha->buha", grad_scores, query_rows, preferred_element_type=jnp.float32)
        .astype(jnp.bfloat16)
        .reshape(replicas * src_len, local_width)
    )
    value_grad = (
        jnp.einsum("bhut,btha->buha", probs_low, grad_rows, preferred_element_type=jnp.float32)
        .astype(jnp.bfloat16)
        .reshape(replicas * src_len, local_width)
    )
    both_grads = jnp.concatenate([key_grad, value_grad], axis=1)
    weight_grads = (
        lax.dot_general(
            all_memory, both_grads, (((0,), (0,)), ((), ())), preferred_element_type=jnp.float32
        )
        * is_decoder
    ).astype(jnp.bfloat16)
    query_back = lax.all_to_all(query_grad_heads, "dp", split_axis=0, concat_axis=1, tiled=True)
    query_grad = (query_back.astype(jnp.float32) * is_decoder).astype(jnp.bfloat16)[None]
    section_part = lax.psum_scatter(
        (
            lax.dot_general(
                both_grads, w_both, (((1,), (1,)), ((), ())), preferred_element_type=jnp.float32
            )
            * is_decoder
        ).astype(jnp.bfloat16),
        "dp",
        scatter_dimension=0,
        tiled=True,
    )
    memory_grad = lax.psum(section_part, "section").astype(jnp.float32)
    scaled_grad = memory_grad * final_gain
    last_grad = inverse * (
        scaled_grad - normed * jnp.mean(scaled_grad * normed, axis=1, keepdims=True)
    )
    state_grad = (last_grad * is_last).astype(jnp.bfloat16)[None]
    gain_grad = lax.psum(jnp.sum(memory_grad * normed, axis=0) * is_last, ("section", "dp"))
    key_weight_grad = weight_grads[:, :local_width][None]
    value_weight_grad = weight_grads[:, local_width:][None]
    return (query_grad, key_weight_grad, value_weight_grad, state_grad, gain_grad)


def solution(mesh):
    placed = (
        P("section", "dp", None),
        P(),
        P("section", "dp", None),
        P("section", None, "dp"),
        P("section", None, "dp"),
        P("section", "dp", None),
        P("dp"),
    )
    return jax.shard_map(
        on_device,
        mesh=mesh,
        in_specs=placed,
        out_specs=(
            P("section", "dp", None),
            P("section", None, "dp"),
            P("section", None, "dp"),
            P("section", "dp", None),
            P(),
        ),
        check_vma=False,
    )
```

profile of v0, /device:TPU:1, one launch (start us, length us, event | category | flops | bytes accessed | tf_op | source)
XLA Modules:
  0.0 639.9 jit_solution(12333519288310503521)
XLA Ops:
  7.2 1.2 fusion.28
  8.4 1.8 fusion.33
  10.3 156.1 %all-reduce.4.cloned.1.call-done = bf16[32,4096]{1,0:T(8,128)(2,1)} async-done(((bf16[32,4096]{1,0:T(8,128)(2,1)}), bf16[32,4096]{1,0:T(8,128)(2,1)}) %all-reduce.4.cloned.1.call-update) | async-done | bytes 262160 | tf_op jit(solution)/shard_map/psum | solution.py:12
  166.4 1.6 copy.13
  168.0 1.3 copy.14
  169.3 19.1 %all-to-all-start = ((bf16[128,16,256]{2,0,1:T(8,128)(2,1)}), bf16[128,16,256]{2,0,1:T(8,128)(2,1)S(1)}, u32[]{:S(2)}, u32[]{:S(2)}) async-start(bf16[128,16,256]{2,0,1:T(8,128)(2,1)} %copy.14), calls=%async_computation | async-start | bytes 2097152 | tf_op jit(solution)/shard_map/all_to_all | solution.py:41
  189.1 1.3 copy.16
  190.4 26.1 %all-to-all-done = bf16[128,16,256]{2,0,1:T(8,128)(2,1)S(1)} async-done(((bf16[128,16,256]{2,0,1:T(8,128)(2,1)}), bf16[128,16,256]{2,0,1:T(8,128)(2,1)S(1)}, u32[]{:S(2)}, u32[]{:S(2)}) %all-to-all-start) | async-done | bytes 1048608 | tf_op jit(solution)/shard_map/all_to_all | solution.py:41
  216.5 7.5 %all-to-all-start.1 = ((bf16[128,16,256]{2,0,1:T(8,128)(2,1)}), bf16[128,16,256]{2,0,1:T(8,128)(2,1)S(1)}, u32[]{:S(2)}, u32[]{:S(2)}) async-start(bf16[128,16,256]{2,0,1:T(8,128)(2,1)} %copy.16), calls=%async_computation.1 | async-start | bytes 2097152 | tf_op jit(solution)/shard_map/all_to_all | solution.py:42
  225.3 0.8 dynamic-update-slice
  226.0 33.3 %all-reduce = s32[16]{0:T(128)S(1)} all-reduce(s32[16]{0:T(128)S(1)} %dynamic-update-slice), channel_id=1, replica_groups=mesh['section'=16,'dp'=16] {'dp'}, use_global_device_ids=true, to_apply=%add | all-reduce | flops 16 | bytes 128
  259.4 15.6 %all-gather.2.cloned.1.call-done = bf16[512,4096]{1,0:T(8,128)(2,1)} async-done(((bf16[32,4096]{1,0:T(8,128)(2,1)}), bf16[512,4096]{1,0:T(8,128)(2,1)}) %all-gather.2.cloned.1.call-update) | async-done | bytes 4194320 | tf_op jit(solution)/shard_map/all_gather | solution.py:33
  275.0 5.8 fusion.4
  283.0 6.6 %multiply_convert_fusion = bf16[512,4096]{1,0:T(8,128)(2,1)} fusion(f32[]{:T(128)S(6)} %convert_element_type.108, bf16[4096,256]{1,0:T(8,128)(2,1)} %bitcast.67, bf16[4096,256]{1,0:T(8,128)(2,1)} %bitcast.69, bf16[512,256]{1,0:T(8,128)(2,1)S(1)} %bitcast.70, bf16[512,256]{1,0:T(8,128)(2,1)S(1)} %bitcast.72), kind=kOutput, calls=%fused_computation.2 | convolution fusion | flops 2161115136 | bytes 8912900 | tf_op jit(solution)/shard_map/dot_general | solution.py:87
  289.6 1.5 fusion.3
  291.1 3.7 all-to-all-start.2
  294.8 4.6 multiply_convert_fusion.1
  299.4 2.3 slice_bitcast_fusion
  301.7 91.4 %reduce-scatter.2.cloned.1.call-done = bf16[32,4096]{1,0:T(8,128)(2,1)} async-done(((bf16[512,4096]{1,0:T(8,128)(2,1)}), bf16[32,4096]{1,0:T(8,128)(2,1)}) %reduce-scatter.2.cloned.1.call-update) | async-done | bytes 262160 | tf_op jit(solution)/shard_map/reduce_scatter | solution.py:85
  393.5 1.3 copy.17
  394.8 150.1 %all-reduce.6.cloned.1.call-done = bf16[32,4096]{1,0:T(8,128)(2,1)} async-done(((bf16[32,4096]{1,0:T(8,128)(2,1)}), bf16[32,4096]{1,0:T(8,128)(2,1)}) %all-reduce.6.cloned.1.call-update) | async-done | bytes 262160 | tf_op jit(solution)/shard_map/psum | solution.py:96
  544.9 1.3 fusion.27
  546.2 85.3 %psum.23 = f32[4096]{0:T(1024)} all-reduce(f32[4096]{0:T(1024)S(1)} %broadcast_multiply_fusion), channel_id=1, replica_groups=mesh['section'=16,'dp'=16] {'section','dp'}, use_global_device_ids=true, to_apply=%region_9.10 | all-reduce | flops 4096 | bytes 32768 | tf_op jit(solution)/shard_map/psum | solution.py:102
  631.5 1.8 fusion.34
  (32 shorter events, 4.0 us)
Async XLA Ops:
  7.2 181.2 %copy-start.1 = (bf16[1,128,4096]{2,1,0:T(8,128)(2,1)S(1)}, bf16[1,128,4096]{2,1,0:T(8,128)(2,1)}, u32[]{:S(2)}) copy-start(bf16[1,128,4096]{2,1,0:T(8,128)(2,1)} %param.12) | copy-start | bytes 3145732
  7.2 159.2 %all-reduce.4.cloned.1.call-start = ((), (), s32[]{:S(2)}) async-start(), calls=%async_computation.4 | async-start | bytes 524288 | tf_op jit(solution)/shard_map/psum | solution.py:12
  10.3 264.7 %all-gather.2.cloned.1.call-start = ((), (), s32[]{:S(2)}) async-start(), calls=%async_computation.5 | async-start | bytes 4456448 | tf_op jit(solution)/shard_map/all_gather | solution.py:33
  169.3 55.3 %copy-start.3 = (u32[256]{0:T(256)S(1)}, u32[256]{0:T(256)}, u32[]{:S(2)}) copy-start(u32[256]{0:T(256)} %constant.31) | copy-start | bytes 3076
  169.3 47.2 %all-to-all-start = ((bf16[128,16,256]{2,0,1:T(8,128)(2,1)}), bf16[128,16,256]{2,0,1:T(8,128)(2,1)S(1)}, u32[]{:S(2)}, u32[]{:S(2)}) async-start(bf16[128,16,256]{2,0,1:T(8,128)(2,1)} %copy.14), calls=%async_computation | async-start | bytes 2097152 | tf_op jit(solution)/shard_map/all_to_all | solution.py:41
  216.5 65.4 %all-to-all-start.1 = ((bf16[128,16,256]{2,0,1:T(8,128)(2,1)}), bf16[128,16,256]{2,0,1:T(8,128)(2,1)S(1)}, u32[]{:S(2)}, u32[]{:S(2)}) async-start(bf16[128,16,256]{2,0,1:T(8,128)(2,1)} %copy.16), calls=%async_computation.1 | async-start | bytes 2097152 | tf_op jit(solution)/shard_map/all_to_all | solution.py:42
  224.0 169.2 %reduce-scatter.2.cloned.1.call-start = ((), (), s32[]{:S(2)}) async-start(), calls=%async_computation.6 | async-start | bytes 4456448 | tf_op jit(solution)/shard_map/reduce_scatter | solution.py:85
  291.1 102.1 %all-to-all-start.2 = ((bf16[16,128,256]{1,2,0:T(8,128)(2,1)}), bf16[16,128,256]{1,2,0:T(8,128)(2,1)S(1)}, u32[]{:S(2)}, u32[]{:S(2)}) async-start(bf16[16,128,256]{1,2,0:T(8,128)(2,1)} %fusion.3), calls=%async_computation.2 | async-start | bytes 2097152 | tf_op jit(solution)/shard_map/all_to_all | solution.py:83
  294.8 250.1 %all-reduce.6.cloned.1.call-start = ((), (), s32[]{:S(2)}) async-start(), calls=%async_computation.7 | async-start | bytes 524288 | tf_op jit(solution)/shard_map/psum | solution.py:96
  301.7 243.2 %copy-start = (bf16[1,32,4096]{2,1,0:T(8,128)(2,1)S(1)}, bf16[1,32,4096]{2,1,0:T(8,128)(2,1)}, u32[]{:S(2)}) copy-start(bf16[1,32,4096]{2,1,0:T(8,128)(2,1)} %param.7) | copy-start | bytes 786436
  301.7 243.2 %copy-start.2 = (f32[4096]{0:T(1024)S(1)}, f32[4096]{0:T(1024)}, u32[]{:S(2)}) copy-start(f32[4096]{0:T(1024)} %param.8) | copy-start | bytes 49156
Sparse Core Ops, SparseCore 0:
  11.2 155.1 all-reduce.3
  169.1 105.8 all-gather.1
  289.7 103.3 reduce-scatter.1
  395.6 149.2 all-reduce.5
where the time goes:
time: 640 us
  waiting for transfers between devices  439 us (69%)
  blocking collectives  119 us (19%)
  starting transfers between devices  30.4 us (5%)
  matrix products  19.9 us (3%)
  between operations  14.6 us (2%)
  local copies, waits for them, and re-layouts  9.89 us (2%)
  other arithmetic  7.1 us (1%)
    psum x1, waiting for transfers between devices, broadcast(): return lax.psum(block, axis)  156 us
    psum x1, waiting for transfers between devices, on_device(): memory_grad = lax.psum(section_part, 'section').astype(jnp.float32)  150 us
    reduce_scatter x1, waiting for transfers between devices, on_device(): lax.psum_scatter((lax.dot_general(both_grads, w_both, (((1,), (1,)), ((),...  91.4 us
    psum x1, blocking collectives, on_device(): lax.psum(jnp.sum(memory_grad * normed, axis=0) * is_last, ('section', 'dp'))  85.3 us
    unnamed x1, blocking collectives  33.3 us
    all_to_all x1, waiting for transfers between devices, on_device(): lax.all_to_all(queries[0], 'dp', split_axis=1, concat_axis=0, tiled=True)  26.1 us
    all_to_all x1, starting transfers between devices, on_device(): lax.all_to_all(queries[0], 'dp', split_axis=1, concat_axis=0, tiled=True)  19.1 us
    all_gather x1, waiting for transfers between devices, on_device(): lax.all_gather(sent, 'dp', axis=0, tiled=True)  15.6 us
  transfers between devices with their start and end apart: 7, of which 5 were waited for; matrix products, arithmetic and copies ran while one was open for 4% of the time, Pallas kernels for 0%

commit v1 on v0

--- a/solution.py
+++ b/solution.py
@@ -99,7 +99,8 @@
         scaled_grad - normed * jnp.mean(scaled_grad * normed, axis=1, keepdims=True)
     )
     state_grad = (last_grad * is_last).astype(jnp.bfloat16)[None]
-    gain_grad = lax.psum(jnp.sum(memory_grad * normed, axis=0) * is_last, ("section", "dp"))
+    inner = lax.psum(jnp.sum(memory_grad * normed, axis=0) * is_last, "section")
+    gain_grad = lax.psum(inner, "dp")
     key_weight_grad = weight_grads[:, :local_width][None]
     value_weight_grad = weight_grads[:, local_width:][None]
     return (query_grad, key_weight_grad, value_weight_grad, state_grad, gain_grad)

time: 640 us -> 726 us (1.13)
  blocking collectives: 119 us -> 199 us
    psum x1 -> x2, blocking collectives: 85.3 us -> 166 us  [the longest x1 101 us: on_device(): gain_grad = lax.psum(inner, 'dp')]
  transfers between devices with their start and end apart: 7 -> 7, of which waited for: 5 -> 5; matrix products, arithmetic and copies ran while one was open for 4% -> 3% of each run, Pallas kernels for 0% -> 0%
where the time goes in v1:
time: 726 us; the launch traced here: 720 us
  waiting for transfers between devices  439 us (60%)
  blocking collectives  199 us (27%)
  starting transfers between devices  30.4 us (4%)
  matrix products  19.9 us (3%)
  between operations  14.6 us (2%)
  local copies, waits for them, and re-layouts  9.89 us (1%)
    psum x1, waiting for transfers between devices, broadcast(): return lax.psum(block, axis)  156 us
    psum x1, waiting for transfers between devices, on_device(): memory_grad = lax.psum(section_part, 'section').astype(jnp.float32)  150 us
    psum x1, blocking collectives, on_device(): gain_grad = lax.psum(inner, 'dp')  101 us
    reduce_scatter x1, waiting for transfers between devices, on_device(): lax.psum_scatter((lax.dot_general(both_grads, w_both, (((1,), (1,)), ((),...  91.4 us
    psum x1, blocking collectives, on_device(): inner = lax.psum(jnp.sum(memory_grad * normed, axis=0) * is_last, 'section')  65.3 us
    unnamed x1, blocking collectives  33.3 us
    all_to_all x1, waiting for transfers between devices, on_device(): lax.all_to_all(queries[0], 'dp', split_axis=1, concat_axis=0, tiled=True)  26.1 us
    all_to_all x1, starting transfers between devices, on_device(): lax.all_to_all(queries[0], 'dp', split_axis=1, concat_axis=0, tiled=True)  19.1 us
  transfers between devices with their start and end apart: 7, of which 5 were waited for; matrix products, arithmetic and copies ran while one was open for 3% of the time, Pallas kernels for 0%

profile of v1, /device:TPU:1, one launch (start us, length us, event | category | flops | bytes accessed | tf_op | source)
XLA Modules:
  0.0 720.4 jit_solution(17861709376003074250)
XLA Ops:
  7.2 1.2 fusion.28
  8.4 1.8 fusion.33
  10.3 156.1 %all-reduce.4.cloned.1.call-done = bf16[32,4096]{1,0:T(8,128)(2,1)} async-done(((bf16[32,4096]{1,0:T(8,128)(2,1)}), bf16[32,4096]{1,0:T(8,128)(2,1)}) %all-reduce.4.cloned.1.call-update) | async-done | bytes 262160 | tf_op jit(solution)/shard_map/psum | solution.py:12
  166.4 1.6 copy.13
  168.0 1.3 copy.14
  169.3 19.1 %all-to-all-start = ((bf16[128,16,256]{2,0,1:T(8,128)(2,1)}), bf16[128,16,256]{2,0,1:T(8,128)(2,1)S(1)}, u32[]{:S(2)}, u32[]{:S(2)}) async-start(bf16[128,16,256]{2,0,1:T(8,128)(2,1)} %copy.14), calls=%async_computation | async-start | bytes 2097152 | tf_op jit(solution)/shard_map/all_to_all | solution.py:41
  189.1 1.3 copy.16
  190.4 26.1 %all-to-all-done = bf16[128,16,256]{2,0,1:T(8,128)(2,1)S(1)} async-done(((bf16[128,16,256]{2,0,1:T(8,128)(2,1)}), bf16[128,16,256]{2,0,1:T(8,128)(2,1)S(1)}, u32[]{:S(2)}, u32[]{:S(2)}) %all-to-all-start) | async-done | bytes 1048608 | tf_op jit(solution)/shard_map/all_to_all | solution.py:41
  216.5 7.5 %all-to-all-start.1 = ((bf16[128,16,256]{2,0,1:T(8,128)(2,1)}), bf16[128,16,256]{2,0,1:T(8,128)(2,1)S(1)}, u32[]{:S(2)}, u32[]{:S(2)}) async-start(bf16[128,16,256]{2,0,1:T(8,128)(2,1)} %copy.16), calls=%async_computation.1 | async-start | bytes 2097152 | tf_op jit(solution)/shard_map/all_to_all | solution.py:42
  226.0 33.3 %all-reduce = s32[16]{0:T(128)S(1)} all-reduce(s32[16]{0:T(128)S(1)} %dynamic-update-slice), channel_id=1, replica_groups=mesh['section'=16,'dp'=16] {'dp'}, use_global_device_ids=true, to_apply=%add | all-reduce | flops 16 | bytes 128
  259.4 15.6 %all-gather.2.cloned.1.call-done = bf16[512,4096]{1,0:T(8,128)(2,1)} async-done(((bf16[32,4096]{1,0:T(8,128)(2,1)}), bf16[512,4096]{1,0:T(8,128)(2,1)}) %all-gather.2.cloned.1.call-update) | async-done | bytes 4194320 | tf_op jit(solution)/shard_map/all_gather | solution.py:33
  275.0 5.8 fusion.4
  283.0 6.6 multiply_convert_fusion
  289.6 1.5 fusion.3
  291.1 3.7 all-to-all-start.2
  294.8 4.6 multiply_convert_fusion.1
  299.4 2.3 slice_bitcast_fusion
  301.7 91.4 %reduce-scatter.2.cloned.1.call-done = bf16[32,4096]{1,0:T(8,128)(2,1)} async-done(((bf16[512,4096]{1,0:T(8,128)(2,1)}), bf16[32,4096]{1,0:T(8,128)(2,1)}) %reduce-scatter.2.cloned.1.call-update) | async-done | bytes 262160 | tf_op jit(solution)/shard_map/reduce_scatter | solution.py:85
  393.5 1.3 copy.17
  394.8 150.1 %all-reduce.6.cloned.1.call-done = bf16[32,4096]{1,0:T(8,128)(2,1)} async-done(((bf16[32,4096]{1,0:T(8,128)(2,1)}), bf16[32,4096]{1,0:T(8,128)(2,1)}) %all-reduce.6.cloned.1.call-update) | async-done | bytes 262160 | tf_op jit(solution)/shard_map/psum | solution.py:96
  544.9 1.3 fusion.27
  546.2 65.3 %psum.30 = f32[4096]{0:T(1024)S(1)} all-reduce(f32[4096]{0:T(1024)S(1)} %broadcast_multiply_fusion), channel_id=1, replica_groups=mesh['section'=16,'dp'=16] {'section'}, use_global_device_ids=true, to_apply=%region_9.10 | all-reduce | flops 4096 | bytes 32768 | tf_op jit(solution)/shard_map/psum | solution.py:102
  611.4 100.6 %psum.31 = f32[4096]{0:T(1024)} all-reduce(f32[4096]{0:T(1024)S(1)} %psum.30), channel_id=1, replica_groups=mesh['section'=16,'dp'=16] {'dp'}, use_global_device_ids=true, to_apply=%region_10.11 | all-reduce | flops 4096 | bytes 32768 | tf_op jit(solution)/shard_map/psum | solution.py:103
  712.0 1.8 fusion.34
  (33 shorter events, 4.8 us)
Async XLA Ops:
  7.2 181.2 %copy-start.1 = (bf16[1,128,4096]{2,1,0:T(8,128)(2,1)S(1)}, bf16[1,128,4096]{2,1,0:T(8,128)(2,1)}, u32[]{:S(2)}) copy-start(bf16[1,128,4096]{2,1,0:T(8,128)(2,1)} %param.12) | copy-start | bytes 3145732
  7.2 159.2 %all-reduce.4.cloned.1.call-start = ((), (), s32[]{:S(2)}) async-start(), calls=%async_computation.4 | async-start | bytes 524288 | tf_op jit(solution)/shard_map/psum | solution.py:12
  10.3 264.7 %all-gather.2.cloned.1.call-start = ((), (), s32[]{:S(2)}) async-start(), calls=%async_computation.5 | async-start | bytes 4456448 | tf_op jit(solution)/shard_map/all_gather | solution.py:33
  169.3 55.3 %copy-start.3 = (u32[256]{0:T(256)S(1)}, u32[256]{0:T(256)}, u32[]{:S(2)}) copy-start(u32[256]{0:T(256)} %constant.31) | copy-start | bytes 3076
  169.3 47.2 %all-to-all-start = ((bf16[128,16,256]{2,0,1:T(8,128)(2,1)}), bf16[128,16,256]{2,0,1:T(8,128)(2,1)S(1)}, u32[]{:S(2)}, u32[]{:S(2)}) async-start(bf16[128,16,256]{2,0,1:T(8,128)(2,1)} %copy.14), calls=%async_computation | async-start | bytes 2097152 | tf_op jit(solution)/shard_map/all_to_all | solution.py:41
  216.5 65.4 %all-to-all-start.1 = ((bf16[128,16,256]{2,0,1:T(8,128)(2,1)}), bf16[128,16,256]{2,0,1:T(8,128)(2,1)S(1)}, u32[]{:S(2)}, u32[]{:S(2)}) async-start(bf16[128,16,256]{2,0,1:T(8,128)(2,1)} %copy.16), calls=%async_computation.1 | async-start | bytes 2097152 | tf_op jit(solution)/shard_map/all_to_all | solution.py:42
  224.0 169.2 %reduce-scatter.2.cloned.1.call-start = ((), (), s32[]{:S(2)}) async-start(), calls=%async_computation.6 | async-start | bytes 4456448 | tf_op jit(solution)/shard_map/reduce_scatter | solution.py:85
  291.1 102.1 %all-to-all-start.2 = ((bf16[16,128,256]{1,2,0:T(8,128)(2,1)}), bf16[16,128,256]{1,2,0:T(8,128)(2,1)S(1)}, u32[]{:S(2)}, u32[]{:S(2)}) async-start(bf16[16,128,256]{1,2,0:T(8,128)(2,1)} %fusion.3), calls=%async_computation.2 | async-start | bytes 2097152 | tf_op jit(solution)/shard_map/all_to_all | solution.py:83
  294.8 250.1 %all-reduce.6.cloned.1.call-start = ((), (), s32[]{:S(2)}) async-start(), calls=%async_computation.7 | async-start | bytes 524288 | tf_op jit(solution)/shard_map/psum | solution.py:96
  301.7 243.2 %copy-start = (bf16[1,32,4096]{2,1,0:T(8,128)(2,1)S(1)}, bf16[1,32,4096]{2,1,0:T(8,128)(2,1)}, u32[]{:S(2)}) copy-start(bf16[1,32,4096]{2,1,0:T(8,128)(2,1)} %param.7) | copy-start | bytes 786436
  301.7 243.2 %copy-start.2 = (f32[4096]{0:T(1024)S(1)}, f32[4096]{0:T(1024)}, u32[]{:S(2)}) copy-start(f32[4096]{0:T(1024)} %param.8) | copy-start | bytes 49156
Sparse Core Ops, SparseCore 0:
  11.2 155.1 all-reduce.3
  169.1 105.8 all-gather.1
  289.7 103.3 reduce-scatter.1
  395.6 149.2 all-reduce.5
